TPU v7x, 32 devices: a whole 2x2x4 slice. The times are simulated.
32 devices in a mesh: row: 8 (over z, x), col: 4 (over y, core).
Axes of the slice: x: 2, y: 2, z: 4, core: 2. Of those that a mesh axis runs over, the one named last changes fastest.
Arguments:
- training_input: float32 [256, 16384], P(None, 'row'), may hold values from -6 to 6
- query_cotangent: float32 [256, 16384], P(None, 'col'), may hold values from -6 to 6
- training_attention: float32 [256, 16384], P(None, 'col'), may hold values from -6 to 6
- output_cotangent: float32 [256, 16384], P(None, 'row'), may hold values from -6 to 6
- rollout_input: bfloat16 [512, 16384], P(None, 'row'), may hold values from -6 to 6
- query_weight: bfloat16 [16384, 16384], P('row', 'col'), may hold values from -0.046875 to 0.046875
- output_weight: bfloat16 [16384, 16384], P('col', 'row'), may hold values from -0.046875 to 0.046875
- cache_keys: bfloat16 [1024, 1024], P('row', 'col'), may hold values from -400 to 400
- cache_values: bfloat16 [1024, 1024], P('row', 'col'), may hold values from -96 to 96
- query_left: float32 [16384, 256], P('row', 'col'), may hold values from -6 to 6
- query_right: float32 [256, 16384], P('row', 'col'), may hold values from -6 to 6
- output_left: float32 [16384, 256], P('col', 'row'), may hold values from -6 to 6
- output_right: float32 [256, 16384], P('col', 'row'), may hold values from -6 to 6
- query_left_moment: float32 [16384, 256], P('row', 'col'), may hold values from -1.75 to 1.75
- query_left_square: float32 [16384, 256], P('row', 'col'), may hold values from 0.001 to 0.01
- query_right_moment: float32 [256, 16384], P('row', 'col'), may hold values from -1.75 to 1.75
- query_right_square: float32 [256, 16384], P('row', 'col'), may hold values from 0.001 to 0.01
- output_left_moment: float32 [16384, 256], P('col', 'row'), may hold values from -1.75 to 1.75
- output_left_square: float32 [16384, 256], P('col', 'row'), may hold values from 0.001 to 0.01
- output_right_moment: float32 [256, 16384], P('col', 'row'), may hold values from -1.75 to 1.75
- output_right_square: float32 [256, 16384], P('col', 'row'), may hold values from 0.001 to 0.01
Outputs:
- stepped_query_left: float32 [16384, 256], P('row', 'col')
- new_query_right: float32 [256, 16384], P('row', 'col')
- new_output_left: float32 [16384, 256], P('col', 'row')
- stepped_output_right: float32 [256, 16384], P('col', 'row')
- rollout_output: float32 [512, 16384], P('col', 'row')
All inputs are finite; a program needn't handle non-finite values.
Results may differ from a plain program's by a relative error of at most 0.0055.
The roundings to bfloat16 on the way count: a program that leaves them out, or rounds other values in their place, can miss the bound.
Values may be sent and summed in bfloat16 or wider, within the bound.
A program may use at most 192 MiB of HBM per device.

v0:
```python
import math

import jax
import jax.numpy as jnp
from jax import lax
from jax.sharding import PartitionSpec as P

MODEL_WIDTH = 16384
HEAD_DIM = 128
FACTOR_RANK = 256


highest = lax.Precision.HIGHEST
learn_rate = 0.03
beta_first = 0.9
beta_second = 0.999
epsilon = 1e-08
weight_decay = 0.1
first_corr = 1.0 - 0.9**50 * 0.9**50
second_corr = 1.0 - 0.999**50 * 0.999**50


def exact_matrix_product(left, right):
    return jnp.dot(left, right, precision=highest, preferred_element_type=jnp.float32)


def adamw_update(factor, gradient, moment, square):
    moment = beta_first * moment + (1.0 - beta_first) * gradient
    square = beta_second * square + (1.0 - beta_second) * gradient * gradient
    change = (
        moment / first_corr / (jnp.sqrt(square / second_corr) + epsilon) + weight_decay * factor
    )
    return factor - learn_rate * change


def attend(query_rows, keys_all, values_all, heads_local):
    total_rows = query_rows.shape[0]
    head_dim = keys_all.shape[1] // heads_local
    group_size = query_rows.shape[1] // keys_all.shape[1]
    row_block = math.gcd(total_rows, 128)
    grouped = query_rows.reshape(
        total_rows // row_block, row_block, heads_local, group_size, head_dim
    )
    keys_three = keys_all.reshape(keys_all.shape[0], heads_local, head_dim)
    values_three = values_all.reshape(values_all.shape[0], heads_local, head_dim)

    def one_block(queries):
        scores = jnp.einsum(
            "bkgd,ckd->bkgc", queries, keys_three, preferred_element_type=jnp.float32
        ) * head_dim ** (-0.5)
        highest_score = jnp.max(scores, axis=-1, keepdims=True)
        exponent = jnp.exp(scores - highest_score)
        weights = (exponent / jnp.sum(exponent, axis=-1, keepdims=True)).astype(jnp.bfloat16)
        mixture = jnp.einsum(
            "bkgc,ckd->bkgd", weights, values_three, preferred_element_type=jnp.float32
        )
        return mixture.astype(jnp.bfloat16)

    blocks = lax.map(one_block, grouped)
    return blocks.reshape(total_rows, heads_local * group_size * head_dim)


def local(
    training_input,
    query_cotangent,
    training_attention,
    output_cotangent,
    rollout_input,
    query_weight,
    output_weight,
    cache_keys,
    cache_values,
    query_left,
    query_right,
    output_left,
    output_right,
    query_left_moment,
    query_left_square,
    query_right_moment,
    query_right_square,
    output_left_moment,
    output_left_square,
    output_right_moment,
    output_right_square,
):
    adapter_scale = 1.0 / math.sqrt(MODEL_WIDTH * FACTOR_RANK)
    row_count = lax.axis_size("row")
    col_count = lax.axis_size("col")
    rank_row = FACTOR_RANK // row_count
    rank_col = FACTOR_RANK // col_count
    row_index = lax.axis_index("row")
    col_index = lax.axis_index("col")
    cotan_part = exact_matrix_product(query_cotangent, query_right.T)
    attn_part = exact_matrix_product(training_attention, output_left)
    cotan_mine, attn_mine = lax.psum((cotan_part, attn_part), "col")
    cotan_every, attn_every = (
        lax.all_gather(cotan_mine, "row", axis=1, tiled=True),
        lax.all_gather(attn_mine, "row", axis=1, tiled=True),
    )
    cotangent_columns = lax.dynamic_slice_in_dim(cotan_every, col_index * rank_col, rank_col, 1)
    attention_columns = lax.dynamic_slice_in_dim(attn_every, col_index * rank_col, rank_col, 1)
    input_part = exact_matrix_product(training_input, query_left)
    outcot_part = exact_matrix_product(output_cotangent, output_right.T)
    input_mine, outcot_mine = lax.psum((input_part, outcot_part), "row")
    input_every, outcot_every = (
        lax.all_gather(input_mine, "col", axis=1, tiled=True),
        lax.all_gather(outcot_mine, "col", axis=1, tiled=True),
    )
    input_row_block = lax.dynamic_slice_in_dim(input_every, row_index * rank_row, rank_row, 1)
    output_cotangent_rows = lax.dynamic_slice_in_dim(
        outcot_every, row_index * rank_row, rank_row, 1
    )
    query_left_gradient = adapter_scale * exact_matrix_product(training_input.T, cotangent_columns)
    query_right_gradient = adapter_scale * exact_matrix_product(input_row_block.T, query_cotangent)
    output_left_gradient = adapter_scale * exact_matrix_product(
        training_attention.T, output_cotangent_rows
    )
    output_right_gradient = adapter_scale * exact_matrix_product(
        attention_columns.T, output_cotangent
    )
    stepped_query_left = adamw_update(
        query_left, query_left_gradient, query_left_moment, query_left_square
    )
    new_query_right = adamw_update(
        query_right, query_right_gradient, query_right_moment, query_right_square
    )
    new_output_left = adamw_update(
        output_left, output_left_gradient, output_left_moment, output_left_square
    )
    stepped_output_right = adamw_update(
        output_right, output_right_gradient, output_right_moment, output_right_square
    )
    next_query_left, next_output_right = (
        lax.all_gather(stepped_query_left, "col", axis=1, tiled=True),
        lax.all_gather(stepped_output_right, "col", axis=0, tiled=True),
    )
    next_query_right, next_output_left = (
        lax.all_gather(new_query_right, "row", axis=0, tiled=True),
        lax.all_gather(new_output_left, "row", axis=1, tiled=True),
    )
    merged_query = (
        query_weight.astype(jnp.float32)
        + adapter_scale * exact_matrix_product(next_query_left, next_query_right)
    ).astype(jnp.bfloat16)
    merged_output = (
        output_weight.astype(jnp.float32)
        + adapter_scale * exact_matrix_product(next_output_left, next_output_right)
    ).astype(jnp.bfloat16)
    keys_all, values_all = (
        lax.all_gather(cache_keys, "row", axis=0, tiled=True),
        lax.all_gather(cache_values, "row", axis=0, tiled=True),
    )
    heads_local = cache_keys.shape[1] // HEAD_DIM
    query_total = lax.psum(
        jnp.dot(rollout_input, merged_query, preferred_element_type=jnp.float32), "row"
    )
    attended = attend(query_total.astype(jnp.bfloat16), keys_all, values_all, heads_local)
    rollout_output = lax.psum_scatter(
        jnp.dot(attended, merged_output, preferred_element_type=jnp.float32),
        "col",
        scatter_dimension=0,
        tiled=True,
    )
    return (
        stepped_query_left,
        new_query_right,
        new_output_left,
        stepped_output_right,
        rollout_output,
    )


def solution(mesh):
    placed = (
        P(None, "row"),
        P(None, "col"),
        P(None, "col"),
        P(None, "row"),
        P(None, "row"),
        P("row", "col"),
        P("col", "row"),
        P("row", "col"),
        P("row", "col"),
        P("row", "col"),
        P("row", "col"),
        P("col", "row"),
        P("col", "row"),
        P("row", "col"),
        P("row", "col"),
        P("row", "col"),
        P("row", "col"),
        P("col", "row"),
        P("col", "row"),
        P("col", "row"),
        P("col", "row"),
    )
    return jax.shard_map(
        local,
        mesh=mesh,
        in_specs=placed,
        out_specs=(
            P("row", "col"),
            P("row", "col"),
            P("col", "row"),
            P("col", "row"),
            P("col", "row"),
        ),
        check_vma=False,
    )
```

profile of v0, /device:TPU:0, one launch (start us, length us, event | category | flops | bytes accessed | tf_op | source)
XLA Modules:
  0.0 851.4 jit_solution(12733438557399462075)
XLA Ops:
  7.2 0.0 copy-start
  7.2 0.0 copy-start.5
  7.2 0.0 all-reduce.8.cloned.1.call-start
  7.2 0.0 copy-start.2
  7.3 0.0 copy-start.6
  7.3 6.7 fusion.85
  14.0 0.0 copy-done.5
  14.0 4.3 fusion.88
  18.3 0.0 all-reduce.8.cloned.1.call-update
  18.3 0.0 all-reduce.6.cloned.1.call-start
  18.4 4.3 fusion.86
  22.6 4.4 fusion.87
  27.0 0.0 all-reduce.6.cloned.1.call-update
  27.1 0.0 all-gather.5.cloned.1.call-start
  27.1 25.7 %all-reduce.8.cloned.1.call-done = (f32[256,32]{0,1:T(8,128)}, f32[256,32]{0,1:T(8,128)}) async-done(((f32[256,32]{0,1:T(8,128)}, f32[256,32]{0,1:T(8,128)}), (f32[256,32]{0,1:T(8,128)}, f32[256,32]{0,1:T(8,128)})) %all-reduce.8.cloned.1.call-update) | async-done | bytes 65552 | tf_op jit(solution)/shard_map/psum | solution.py:95
  52.8 31.3 %all_gather.30 = f32[256,256]{0,1:T(8,128)S(1)} all-gather(f32[256,32]{0,1:T(8,128)} %get-tuple-element.60), channel_id=1, replica_groups=mesh['row'=8,'col'=4] {'row'}, dimensions={1}, use_global_device_ids=true | all-gather | bytes 294912 | tf_op jit(solution)/shard_map/all_gather | solution.py:97
  84.1 4.5 fusion.52
  88.6 0.0 all-gather.5.cloned.1.call-update
  88.6 0.0 all-gather.7.cloned.1.call-start
  88.7 38.9 %all-reduce.6.cloned.1.call-done = (f32[256,64]{0,1:T(8,128)}, f32[256,64]{0,1:T(8,128)}) async-done(((f32[256,64]{0,1:T(8,128)}, f32[256,64]{0,1:T(8,128)}), (f32[256,64]{0,1:T(8,128)}, f32[256,64]{0,1:T(8,128)})) %all-reduce.6.cloned.1.call-update) | async-done | bytes 131088 | tf_op jit(solution)/shard_map/psum | solution.py:104
  127.6 6.2 all_gather.31
  133.8 6.3 multiply_subtract_fusion.1
  140.1 0.0 all-gather.7.cloned.1.call-update
  140.1 0.0 all-gather.11.cloned.1.call-start
  140.2 31.4 %all_gather.33 = f32[256,256]{0,1:T(8,128)S(1)} all-gather(f32[256,32]{0,1:T(8,128)S(1)} %copy-done.12), channel_id=1, replica_groups=mesh['row'=8,'col'=4] {'row'}, dimensions={1}, use_global_device_ids=true | all-gather | bytes 294912 | tf_op jit(solution)/shard_map/all_gather | solution.py:98
  171.6 4.5 multiply_subtract_fusion
  176.2 0.0 all-gather.11.cloned.1.call-update
  176.2 0.0 all-gather.9.cloned.1.call-start
  176.3 0.0 copy-done.10
  176.3 0.1 copy.33
  176.4 30.4 %all_gather.36 = bf16[1024,256]{0,1:T(8,128)(2,1)S(1)} all-gather(bf16[128,256]{0,1:T(8,128)(2,1)S(1)} %copy.33), channel_id=1, replica_groups=mesh['row'=8,'col'=4] {'row'}, dimensions={0}, use_global_device_ids=true | all-gather | bytes 589824 | tf_op jit(solution)/shard_map/all_gather | solution.py:150
  206.8 1.0 copy.36
  207.8 0.1 copy.34
  207.9 32.7 %all_gather.37 = bf16[1024,256]{0,1:T(8,128)(2,1)S(1)} all-gather(bf16[128,256]{0,1:T(8,128)(2,1)S(1)} %copy.34), channel_id=1, replica_groups=mesh['row'=8,'col'=4] {'row'}, dimensions={0}, use_global_device_ids=true | all-gather | bytes 589824 | tf_op jit(solution)/shard_map/all_gather | solution.py:151
  240.6 1.0 copy.37
  241.6 5.8 all_gather.32
  247.3 6.0 fusion.44
  253.4 0.0 all-gather.9.cloned.1.call-update
  253.4 0.4 reduce-scatter.2.cloned.1.call-start
  253.9 0.0 all-gather.5.cloned.1.call-done
  253.9 0.0 all-gather.7.cloned.1.call-done
  253.9 32.4 %fusion.89 = f32[2048,4096]{1,0:T(8,128)} fusion(f32[2048,256]{0,1:T(8,128)} %all-gather.5.cloned.1.call-done, f32[256,4096]{1,0:T(8,128)} %all-gather.7.cloned.1.call-done), kind=kOutput, calls=%fused_computation.72 | convolution fusion | flops 25769803776 | bytes 39845888 | tf_op jit(solution)/shard_map/dot_general | solution.py:24
  286.3 21.4 %fusion.37 = f32[512,4096]{0,1:T(8,128)} fusion(bf16[512,2048]{1,0:T(8,128)(2,1)S(1)} %copy-done, f32[2048,4096]{1,0:T(8,128)} %fusion.89, bf16[2048,4096]{1,0:T(8,128)(2,1)} %param.28), kind=kOutput, calls=%fused_computation.30 | convolution fusion | flops 8623489024 | bytes 60817408 | tf_op jit(solution)/shard_map/dot_general | solution.py:155
  307.7 337.2 %all-reduce.9 = bf16[512,4096]{0,1:T(8,128)(2,1)} all-reduce(f32[512,4096]{0,1:T(8,128)} %fusion.37), channel_id=1, replica_groups=mesh['row'=8,'col'=4] {'row'}, use_global_device_ids=true, to_apply=%region_4.0 | all-reduce | flops 2097152 | bytes 12582912 | tf_op jit(solution)/shard_map/psum | solution.py:154
  644.9 6.9 reshape.24
  651.9 7.6 copy.35
  659.4 79.1 %while.10 = (s32[]{:T(128)}, bf16[4,128,2,16,128]{4,3,2,1,0:T(8,128)(2,1)}, bf16[4,128,2,16,128]{4,1,3,2,0:T(8,128)(2,1)}, bf16[1024,2,128]{2,0,1:T(8,128)(2,1)S...) while((s32[]{:T(128)}, bf16[4,128,2,16,128]{4,3,2,1,0:T(8,128)(2,1)}, ...), condition=%wide.region_8.9_spmd, body=%wide.region_5.8_spmd.sunk | while | flops 2168980480 | bytes 38831172 | solution.py:59
  659.4 9.9 %fusion.117 = (f32[128,2,16]{0,2,1:T(8,128)S(1)}, f32[128,2,16,1024]{3,0,2,1:T(8,128)}) fusion(bf16[4,128,2,16,128]{4,1,3,2,0:T(8,128)(2,1)} %get-tuple-element.113, s32[]{:T(128)} %get-tuple-element.105, bf16[1024,2,128]{2,0,1:T(8,128)(2,1)S(1)} %get-tuple-element.114), kind=kOutput, calls=%fused_computation.67.clone.1 | convolution fusion | flops 1086325760 | bytes 18366976 | tf_op jit(solution)/shard_map/while/body/eval_jaxpr/sub | solution.py:52
  669.4 8.2 fusion.118
  677.5 1.7 copy_dynamic-update-slice_fusion.2
  679.2 9.9 %fusion.117 = (f32[128,2,16]{0,2,1:T(8,128)S(1)}, f32[128,2,16,1024]{3,0,2,1:T(8,128)}) fusion(bf16[4,128,2,16,128]{4,1,3,2,0:T(8,128)(2,1)} %get-tuple-element.113, s32[]{:T(128)} %get-tuple-element.105, bf16[1024,2,128]{2,0,1:T(8,128)(2,1)S(1)} %get-tuple-element.114), kind=kOutput, calls=%fused_computation.67.clone.1 | convolution fusion | flops 1086325760 | bytes 18366976 | tf_op jit(solution)/shard_map/while/body/eval_jaxpr/sub | solution.py:52
  689.1 8.2 fusion.118
  697.3 1.7 copy_dynamic-update-slice_fusion.2
  699.0 9.9 %fusion.117 = (f32[128,2,16]{0,2,1:T(8,128)S(1)}, f32[128,2,16,1024]{3,0,2,1:T(8,128)}) fusion(bf16[4,128,2,16,128]{4,1,3,2,0:T(8,128)(2,1)} %get-tuple-element.113, s32[]{:T(128)} %get-tuple-element.105, bf16[1024,2,128]{2,0,1:T(8,128)(2,1)S(1)} %get-tuple-element.114), kind=kOutput, calls=%fused_computation.67.clone.1 | convolution fusion | flops 1086325760 | bytes 18366976 | tf_op jit(solution)/shard_map/while/body/eval_jaxpr/sub | solution.py:52
  708.9 8.2 fusion.118
  717.1 1.7 copy_dynamic-update-slice_fusion.2
  718.7 9.9 %fusion.117 = (f32[128,2,16]{0,2,1:T(8,128)S(1)}, f32[128,2,16,1024]{3,0,2,1:T(8,128)}) fusion(bf16[4,128,2,16,128]{4,1,3,2,0:T(8,128)(2,1)} %get-tuple-element.113, s32[]{:T(128)} %get-tuple-element.105, bf16[1024,2,128]{2,0,1:T(8,128)(2,1)S(1)} %get-tuple-element.114), kind=kOutput, calls=%fused_computation.67.clone.1 | convolution fusion | flops 1086325760 | bytes 18366976 | tf_op jit(solution)/shard_map/while/body/eval_jaxpr/sub | solution.py:52
  728.7 8.2 fusion.118
  736.8 1.7 copy_dynamic-update-slice_fusion.2
  738.5 7.3 reshape.27
  745.8 32.6 %fusion.90 = f32[4096,2048]{1,0:T(8,128)} fusion(f32[4096,256]{0,1:T(8,128)} %all-gather.9.cloned.1.call-done, f32[256,2048]{1,0:T(8,128)} %all-gather.11.cloned.1.call-done), kind=kOutput, calls=%fused_computation.73 | convolution fusion | flops 25769803776 | bytes 39845888 | tf_op jit(solution)/shard_map/dot_general | solution.py:24
  778.5 20.2 %fusion.34 = f32[512,2048]{1,0:T(8,128)} fusion(bf16[512,4096]{1,0:T(8,128)(2,1)S(1)} %copy-done.3, f32[4096,2048]{1,0:T(8,128)} %fusion.90, bf16[4096,2048]{1,0:T(8,128)(2,1)} %param.29), kind=kOutput, calls=%fused_computation.27 | convolution fusion | flops 8623489024 | bytes 58720256 | tf_op jit(solution)/shard_map/dot_general | solution.py:159
  798.7 0.0 reduce-scatter.2.cloned.1.call-update
  798.7 45.7 %reduce-scatter.2.cloned.1.call-done = f32[128,2048]{1,0:T(8,128)} async-done(((f32[512,2048]{1,0:T(8,128)}), f32[128,2048]{1,0:T(8,128)}) %reduce-scatter.2.cloned.1.call-update) | async-done | bytes 1048592 | tf_op jit(solution)/shard_map/reduce_scatter | solution.py:158
  (23 shorter events, 0.0 us)
Async XLA Ops:
  7.2 279.1 %copy-start = (bf16[512,2048]{1,0:T(8,128)(2,1)S(1)}, bf16[512,2048]{1,0:T(8,128)(2,1)}, u32[]{:S(2)}) copy-start(bf16[512,2048]{1,0:T(8,128)(2,1)} %param.27) | copy-start | bytes 6291460
  7.2 6.8 copy-start.5
  7.2 45.6 %all-reduce.8.cloned.1.call-start = ((), (), s32[]{:S(2)}) async-start(), calls=%async_computation.7 | async-start | bytes 131072 | tf_op jit(solution)/shard_map/psum | solution.py:95
  7.2 6.8 copy-start.2
  7.3 11.1 %copy-start.6 = (f32[2048,64]{0,1:T(8,128)S(1)}, f32[2048,64]{0,1:T(8,128)}, u32[]{:S(2)}) copy-start(f32[2048,64]{0,1:T(8,128)} %param.32) | copy-start | bytes 1572868
  18.3 109.3 %all-reduce.6.cloned.1.call-start = ((), (), s32[]{:S(2)}) async-start(), calls=%async_computation.6 | async-start | bytes 262144 | tf_op jit(solution)/shard_map/psum | solution.py:104
  22.6 111.2 %copy-start.4 = (f32[32,4096]{1,0:T(8,128)S(1)}, f32[32,4096]{1,0:T(8,128)}, u32[]{:S(2)}) copy-start(f32[32,4096]{1,0:T(8,128)} %param.33) | copy-start | bytes 1572868
  27.1 226.8 %all-gather.5.cloned.1.call-start = ((), (), s32[]{:S(2)}) async-start(), calls=%async_computation.1 | async-start | bytes 2621440 | tf_op jit(solution)/shard_map/all_gather | solution.py:134
  88.6 51.6 %copy-start.12 = (f32[256,32]{0,1:T(8,128)S(1)}, f32[256,32]{0,1:T(8,128)}, u32[]{:S(2)}) copy-start(f32[256,32]{0,1:T(8,128)} %get-tuple-element.61) | copy-start | bytes 98308
  88.6 165.3 %all-gather.7.cloned.1.call-start = ((), (), s32[]{:S(2)}) async-start(), calls=%async_computation.2 | async-start | bytes 4718592 | tf_op jit(solution)/shard_map/all_gather | solution.py:138
  140.1 36.2 %copy-start.10 = (bf16[128,256]{1,0:T(8,128)(2,1)S(1)}, bf16[128,256]{1,0:T(8,128)(2,1)}, u32[]{:S(2)}) copy-start(bf16[128,256]{1,0:T(8,128)(2,1)} %param.30) | copy-start | bytes 196612
  140.1 67.7 %copy-start.11 = (bf16[128,256]{1,0:T(8,128)(2,1)S(1)}, bf16[128,256]{1,0:T(8,128)(2,1)}, u32[]{:S(2)}) copy-start(bf16[128,256]{1,0:T(8,128)(2,1)} %param.31) | copy-start | bytes 196612
  140.1 605.7 %all-gather.11.cloned.1.call-start = ((), (), s32[]{:S(2)}) async-start(), calls=%async_computation.4 | async-start | bytes 2621440 | tf_op jit(solution)/shard_map/all_gather | solution.py:135
  171.6 70.0 %copy-start.9 = (f32[256,64]{0,1:T(8,128)S(1)}, f32[256,64]{0,1:T(8,128)}, u32[]{:S(2)}) copy-start(f32[256,64]{0,1:T(8,128)} %get-tuple-element.59) | copy-start | bytes 196612
  176.2 569.6 %all-gather.9.cloned.1.call-start = ((), (), s32[]{:S(2)}) async-start(), calls=%async_computation.3 | async-start | bytes 4718592 | tf_op jit(solution)/shard_map/all_gather | solution.py:139
  253.4 591.0 %reduce-scatter.2.cloned.1.call-start = ((), (), s32[]{:S(2)}) async-start(), calls=%async_computation.5 | async-start | bytes 5242880 | tf_op jit(solution)/shard_map/reduce_scatter | solution.py:158
  651.9 7.6 copy-start.7
  651.9 7.6 copy-start.8
  745.8 32.7 %copy-start.3 = (bf16[512,4096]{1,0:T(8,128)(2,1)S(1)}, bf16[512,4096]{1,0:T(8,128)(2,1)}, u32[]{:S(2)}) copy-start(bf16[512,4096]{1,0:T(8,128)(2,1)} %reshape.27) | copy-start | bytes 12582916
  778.5 65.9 %copy-start.1 = (bf16[512,2048]{1,0:T(8,128)(2,1)S(1)}, bf16[512,2048]{1,0:T(8,128)(2,1)}, u32[]{:S(2)}) copy-start(bf16[512,2048]{1,0:T(8,128)(2,1)} %param.27) | copy-start | bytes 6291460
Sparse Core Ops, SparseCore 0:
  18.4 34.3 all-reduce.7
  56.8 70.7 all-reduce.5
  129.8 21.6 all-gather.4
  154.0 86.5 all-gather.6
  242.6 23.6 all-gather.10
  268.8 110.8 all-gather.8
  798.8 45.5 reduce-scatter.1
where the time goes:
time: 860 us; the launch traced here: 851 us
  blocking collectives  475 us (55%)
  matrix products  220 us (26%)
  waiting for transfers between devices  110 us (13%)
  local copies, waits for them, and re-layouts  30.8 us (4%)
  between operations  14.5 us (2%)
    psum x1, blocking collectives, local(): lax.psum(jnp.dot(rollout_input, merged_query, preferred_element_type=jnp....  337 us
    dot_general x10, matrix products, exact_matrix_product(): jnp.dot(left, right, precision=highest, preferred_element_type=jnp.float32)  106 us
    reduce_scatter x1, waiting for transfers between devices, local(): lax.psum_scatter(jnp.dot(attended, merged_output, preferred_element_type=...  45.7 us
    sub x4, matrix products, one_block(): exponent = jnp.exp(scores - highest_score)  39.7 us
    psum x1, waiting for transfers between devices, local(): input_mine, outcot_mine = lax.psum((input_part, outcot_part), 'row')  38.9 us
    dot_general x4, matrix products, one_block(): jnp.einsum('bkgc,ckd->bkgd', weights, values_three, preferred_element_typ...  32.7 us
    all_gather x1, blocking collectives, local(): lax.all_gather(cache_values, 'row', axis=0, tiled=True)  32.7 us
    all_gather x1, blocking collectives, local(): lax.all_gather(attn_mine, 'row', axis=1, tiled=True)  31.4 us
  transfers between devices with their start and end apart: 7, of which 3 were waited for; matrix products, arithmetic and copies ran while one was open for 22% of the time, Pallas kernels for 0%

commit v1 on v0

v1 whole, which is shorter than its diff:
```python
import functools
import math

import jax
import jax.numpy as jnp
from jax import lax
from jax.experimental import pallas as pl
from jax.experimental.pallas import tpu as pltpu
from jax.sharding import PartitionSpec as P

MODEL_WIDTH = 16384
HEAD_DIM = 128
FACTOR_RANK = 256


high = lax.Precision.HIGH
learn_rate = 0.03
beta_first = 0.9
beta_second = 0.999
epsilon = 1e-08
weight_decay = 0.1
first_corr = 1.0 - 0.9**50 * 0.9**50
second_corr = 1.0 - 0.999**50 * 0.999**50


def high_product(left, right):
    return jnp.dot(left, right, precision=high, preferred_element_type=jnp.float32)


def turned_product(left, right):
    return lax.dot_general(
        left,
        right,
        (((1,), (1,)), ((), ())),
        precision=high,
        preferred_element_type=jnp.float32,
    )


def adamw_update(factor, gradient, moment, square):
    moment = beta_first * moment + (1.0 - beta_first) * gradient
    square = beta_second * square + (1.0 - beta_second) * gradient * gradient
    change = (
        moment / first_corr / (jnp.sqrt(square / second_corr) + epsilon) + weight_decay * factor
    )
    return factor - learn_rate * change


def split_pair(value):
    upper = value.astype(jnp.bfloat16)
    return upper, (value - upper.astype(jnp.float32)).astype(jnp.bfloat16)


def merged_block(left_upper, left_lower, right_value, weight, scale):
    right_upper, right_lower = split_pair(right_value)
    delta = jnp.dot(left_upper, right_upper, preferred_element_type=jnp.float32)
    delta += jnp.dot(left_upper, right_lower, preferred_element_type=jnp.float32)
    delta += jnp.dot(left_lower, right_upper, preferred_element_type=jnp.float32)
    return (weight.astype(jnp.float32) + scale * delta).astype(jnp.bfloat16)


def keep_left(left_ref, upper_ref, lower_ref, block):
    @pl.when(pl.program_id(0) == 0)
    def _():
        upper, lower = split_pair(left_ref[...].T)
        upper_ref[block] = upper
        lower_ref[block] = lower


def project_kernel(scale, x_ref, left_ref, right_ref, weight_ref, out_ref, upper_ref, lower_ref):
    block = pl.program_id(1)
    keep_left(left_ref, upper_ref, lower_ref, block)
    merged = merged_block(
        upper_ref[block], lower_ref[block], right_ref[...], weight_ref[...], scale
    )
    part = jnp.dot(x_ref[...], merged, preferred_element_type=jnp.float32)

    @pl.when(block == 0)
    def _():
        out_ref[...] = part

    @pl.when(block > 0)
    def _():
        out_ref[...] += part


def merge_kernel(scale, left_ref, right_ref, weight_ref, out_ref, upper_ref, lower_ref):
    block = pl.program_id(1)
    keep_left(left_ref, upper_ref, lower_ref, block)
    out_ref[...] = merged_block(
        upper_ref[block], lower_ref[block], right_ref[...], weight_ref[...], scale
    )


def left_scratch(blocks, tile, rank):
    return [
        pltpu.VMEM((blocks, tile, rank), jnp.bfloat16),
        pltpu.VMEM((blocks, tile, rank), jnp.bfloat16),
    ]


def project_merged(scale, x, left_turned, right, weight, start, width):
    depth = weight.shape[0]
    rank = right.shape[0]
    rows = x.shape[0]
    tile_depth, tile_width = math.gcd(depth, 512), math.gcd(width, 512)
    blocks = depth // tile_depth
    first = start // tile_width
    return pl.pallas_call(
        functools.partial(project_kernel, scale),
        grid=(width // tile_width, blocks),
        in_specs=[
            pl.BlockSpec((rows, tile_depth), lambda j, k: (0, k)),
            pl.BlockSpec((rank, tile_depth), lambda j, k: (0, jnp.where(j == 0, k, blocks - 1))),
            pl.BlockSpec((rank, tile_width), lambda j, k: (0, first + j)),
            pl.BlockSpec((tile_depth, tile_width), lambda j, k: (k, first + j)),
        ],
        out_specs=pl.BlockSpec((rows, tile_width), lambda j, k: (0, j)),
        out_shape=jax.ShapeDtypeStruct((rows, width), jnp.float32),
        scratch_shapes=left_scratch(blocks, tile_depth, rank),
        compiler_params=pltpu.CompilerParams(
            dimension_semantics=("arbitrary", "arbitrary"), vmem_limit_bytes=32 * 2**20
        ),
        cost_estimate=pl.CostEstimate(
            flops=2 * depth * width * (3 * rank + rows),
            bytes_accessed=2 * depth * width + 4 * rows * width,
            transcendentals=0,
        ),
    )(x, left_turned, right, weight)


def merge_weight(scale, left_turned, right, weight):
    depth, width = weight.shape
    rank = right.shape[0]
    tile_depth, tile_width = math.gcd(depth, 512), math.gcd(width, 512)
    blocks = depth // tile_depth
    return pl.pallas_call(
        functools.partial(merge_kernel, scale),
        grid=(width // tile_width, blocks),
        in_specs=[
            pl.BlockSpec((rank, tile_depth), lambda j, k: (0, jnp.where(j == 0, k, blocks - 1))),
            pl.BlockSpec((rank, tile_width), lambda j, k: (0, j)),
            pl.BlockSpec((tile_depth, tile_width), lambda j, k: (k, j)),
        ],
        out_specs=pl.BlockSpec((tile_depth, tile_width), lambda j, k: (k, j)),
        out_shape=jax.ShapeDtypeStruct((depth, width), jnp.bfloat16),
        scratch_shapes=left_scratch(blocks, tile_depth, rank),
        compiler_params=pltpu.CompilerParams(
            dimension_semantics=("arbitrary", "arbitrary"), vmem_limit_bytes=32 * 2**20
        ),
        cost_estimate=pl.CostEstimate(
            flops=6 * depth * width * rank,
            bytes_accessed=4 * depth * width,
            transcendentals=0,
        ),
    )(left_turned, right, weight)


def attend_kernel(head_dim, q_ref, k_ref, v_ref, out_ref):
    rows, width = q_ref.shape
    heads = width // head_dim
    queries = jnp.concatenate(
        [q_ref[:, h * head_dim : (h + 1) * head_dim] for h in range(heads)], axis=0
    ).astype(jnp.bfloat16)
    scores = lax.dot_general(
        queries, k_ref[...], (((1,), (1,)), ((), ())), preferred_element_type=jnp.float32
    ) * head_dim ** (-0.5)
    exponent = jnp.exp(scores - jnp.max(scores, axis=-1, keepdims=True))
    weights = (exponent / jnp.sum(exponent, axis=-1, keepdims=True)).astype(jnp.bfloat16)
    mixture = jnp.dot(weights, v_ref[...], preferred_element_type=jnp.float32)
    mixture = mixture.astype(jnp.bfloat16)
    for h in range(heads):
        out_ref[:, h * head_dim : (h + 1) * head_dim] = mixture[h * rows : (h + 1) * rows]


def attend(query_rows, keys, values, head, key_heads):
    rows, width = query_rows.shape
    positions = keys.shape[0]
    head_dim = HEAD_DIM
    tile = head_dim * math.gcd(width // head_dim, max(1, 512 // rows))
    return pl.pallas_call(
        functools.partial(attend_kernel, head_dim),
        grid=(width // tile,),
        in_specs=[
            pl.BlockSpec((rows, tile), lambda i: (0, i)),
            pl.BlockSpec((positions, head_dim), lambda i: (0, head)),
            pl.BlockSpec((positions, head_dim), lambda i: (0, key_heads + head)),
        ],
        out_specs=pl.BlockSpec((rows, tile), lambda i: (0, i)),
        out_shape=jax.ShapeDtypeStruct((rows, width), jnp.bfloat16),
        compiler_params=pltpu.CompilerParams(
            dimension_semantics=("arbitrary",), vmem_limit_bytes=32 * 2**20
        ),
        cost_estimate=pl.CostEstimate(
            flops=4 * rows * width * positions,
            bytes_accessed=6 * rows * width + 4 * positions * head_dim,
            transcendentals=rows * width // head_dim * positions,
        ),
    )(query_rows, keys, values)


def local(
    training_input,
    query_cotangent,
    training_attention,
    output_cotangent,
    rollout_input,
    query_weight,
    output_weight,
    cache_keys,
    cache_values,
    query_left,
    query_right,
    output_left,
    output_right,
    query_left_moment,
    query_left_square,
    query_right_moment,
    query_right_square,
    output_left_moment,
    output_left_square,
    output_right_moment,
    output_right_square,
):
    adapter_scale = 1.0 / math.sqrt(MODEL_WIDTH * FACTOR_RANK)
    input_turned = turned_product(query_left.T, training_input)
    outcot_turned = turned_product(output_right, output_cotangent)
    input_every = lax.all_gather(
        jnp.concatenate((input_turned, outcot_turned), axis=1), "col", axis=0, tiled=True
    )
    input_rank = lax.psum_scatter(input_every, "row", scatter_dimension=0, tiled=True)
    cotan_turned = turned_product(query_right, query_cotangent)
    attn_turned = turned_product(output_left.T, training_attention)
    cotan_every = lax.all_gather(
        jnp.concatenate((cotan_turned, attn_turned), axis=1), "row", axis=0, tiled=True
    )
    cotan_rank = lax.psum_scatter(cotan_every, "col", scatter_dimension=0, tiled=True)
    rows = training_input.shape[0]
    query_left_gradient = adapter_scale * high_product(cotan_rank[:, :rows], training_input).T
    query_right_gradient = adapter_scale * high_product(input_rank[:, :rows], query_cotangent)
    output_left_gradient = adapter_scale * high_product(input_rank[:, rows:], training_attention).T
    output_right_gradient = adapter_scale * high_product(cotan_rank[:, rows:], output_cotangent)
    new_query_right = adamw_update(
        query_right, query_right_gradient, query_right_moment, query_right_square
    )
    stepped_query_left = adamw_update(
        query_left, query_left_gradient, query_left_moment, query_left_square
    )
    new_output_left = adamw_update(
        output_left, output_left_gradient, output_left_moment, output_left_square
    )
    stepped_output_right = adamw_update(
        output_right, output_right_gradient, output_right_moment, output_right_square
    )
    next_query_right = lax.all_gather(new_query_right, "row", axis=0, tiled=True)
    next_query_left = lax.all_gather(stepped_query_left.T, "col", axis=0, tiled=True)
    next_output_left = lax.all_gather(new_output_left.T, "row", axis=0, tiled=True)
    next_output_right = lax.all_gather(stepped_output_right, "col", axis=0, tiled=True)
    cache_all = lax.all_gather(
        jnp.concatenate((cache_keys, cache_values), axis=1), "row", axis=0, tiled=True
    )
    key_heads = cache_keys.shape[1] // HEAD_DIM
    width = query_weight.shape[1] // key_heads
    queries = [
        lax.psum_scatter(
            project_merged(
                adapter_scale,
                rollout_input,
                next_query_left,
                next_query_right,
                query_weight,
                head * width,
                width,
            ),
            "row",
            scatter_dimension=0,
            tiled=True,
        )
        for head in range(key_heads)
    ]
    merged_output = merge_weight(
        adapter_scale, next_output_left, next_output_right, output_weight
    )
    attended = [
        lax.all_gather(
            attend(queries[head], cache_all, cache_all, head, key_heads),
            "row",
            axis=0,
            tiled=True,
        )
        for head in range(key_heads)
    ]
    portion = sum(
        jnp.dot(
            attended[head],
            merged_output[head * width : (head + 1) * width],
            preferred_element_type=jnp.float32,
        )
        for head in range(key_heads)
    )
    rollout_output = lax.psum_scatter(portion, "col", scatter_dimension=0, tiled=True)
    return (
        stepped_query_left,
        new_query_right,
        new_output_left,
        stepped_output_right,
        rollout_output,
    )


def solution(mesh):
    placed = (
        P(None, "row"),
        P(None, "col"),
        P(None, "col"),
        P(None, "row"),
        P(None, "row"),
        P("row", "col"),
        P("col", "row"),
        P("row", "col"),
        P("row", "col"),
        P("row", "col"),
        P("row", "col"),
        P("col", "row"),
        P("col", "row"),
        P("row", "col"),
        P("row", "col"),
        P("row", "col"),
        P("row", "col"),
        P("col", "row"),
        P("col", "row"),
        P("col", "row"),
        P("col", "row"),
    )
    return jax.shard_map(
        local,
        mesh=mesh,
        in_specs=placed,
        out_specs=(
            P("row", "col"),
            P("row", "col"),
            P("col", "row"),
            P("col", "row"),
            P("col", "row"),
        ),
        check_vma=False,
    )
```

time: 860 us -> 724 us (0.84)
  blocking collectives: 475 us -> 42.9 us
  waiting for transfers between devices: 110 us -> 512 us
  matrix products: 220 us -> 48.7 us
  Pallas kernels: 0 us -> 81.2 us
  local copies, waits for them, and re-layouts: 30.8 us -> 21.5 us
    psum x1 -> x0, blocking collectives: 337 us -> none  [local(): lax.psum(jnp.dot(rollout_input, merged_query, preferred_element_type=jnp....]
    reduce_scatter x1 -> x5, waiting for transfers between devices: 45.7 us -> 272 us  [the longest x2 155 us: local(): lax.psum_scatter(project_merged(adapter_scale, rollout_input, next_query_...]
    all_gather x2 -> x5, waiting for transfers between devices: 0.02 us -> 147 us  [the longest x1 75.5 us: local(): lax.all_gather(new_output_left.T, 'row', axis=0, tiled=True)]
    dot_general x16 -> x10, matrix products: 180 us -> 48.7 us  [the longest x2 22.2 us: local(): jnp.dot(attended[head], merged_output[head * width:(head + 1) * width], p...]
    all_gather x6 -> x2, blocking collectives: 138 us -> 42.9 us  [the longest x1 35.2 us: local(): lax.all_gather(jnp.concatenate((cotan_turned, attn_turned), axis=1), 'row...]
    pallas_call x0 -> x5, Pallas kernels: none -> 81.2 us  [the longest x2 40.2 us: project_merged(): pl.pallas_call(functools.partial(project_kernel, scale), grid=(width // t...]
    all_gather x1, waiting for transfers between devices: 0.02 us -> 75.4 us  [local(): lax.all_gather(new_query_right, 'row', axis=0, tiled=True)]
    psum x2 -> x0, waiting for transfers between devices: 64.6 us -> none  [the longest x1 38.9 us: local(): input_mine, outcot_mine = lax.psum((input_part, outcot_part), 'row')]
  transfers between devices with their start and end apart: 7 -> 12, of which waited for: 3 -> 11; matrix products, arithmetic and copies ran while one was open for 22% -> 4% of each run, Pallas kernels for 0% -> 11%
where the time goes in v1:
time: 724 us; the launch traced here: 722 us
  waiting for transfers between devices  512 us (71%)
  Pallas kernels  81.2 us (11%)
  matrix products  48.7 us (7%)
  blocking collectives  42.9 us (6%)
  local copies, waits for them, and re-layouts  21.5 us (3%)
  between operations  14.4 us (2%)
    reduce_scatter x2, waiting for transfers between devices, local(): lax.psum_scatter(project_merged(adapter_scale, rollout_input, next_query_...  155 us
    all_gather x1, waiting for transfers between devices, local(): lax.all_gather(new_output_left.T, 'row', axis=0, tiled=True)  75.5 us
    all_gather x1, waiting for transfers between devices, local(): lax.all_gather(new_query_right, 'row', axis=0, tiled=True)  75.4 us
    reduce_scatter x1, waiting for transfers between devices, local(): lax.psum_scatter(input_every, 'row', scatter_dimension=0, tiled=True)  62.7 us
    all_gather x2, waiting for transfers between devices, local(): lax.all_gather(attend(queries[head], cache_all, cache_all, head, key_head...  53.2 us
    reduce_scatter x1, waiting for transfers between devices, local(): lax.psum_scatter(portion, 'col', scatter_dimension=0, tiled=True)  43.3 us
    pallas_call x2, Pallas kernels, project_merged(): pl.pallas_call(functools.partial(project_kernel, scale), grid=(width // t...  40.2 us
    all_gather x1, blocking collectives, local(): lax.all_gather(jnp.concatenate((cotan_turned, attn_turned), axis=1), 'row...  35.2 us
  transfers between devices with their start and end apart: 12, of which 11 were waited for; matrix products, arithmetic and copies ran while one was open for 4% of the time, Pallas kernels for 11%

profile of v1, /device:TPU:0, one launch (start us, length us, event | category | flops | bytes accessed | tf_op | source)
XLA Modules:
  0.0 722.4 jit_solution(646866728488450733)
XLA Ops:
  7.2 0.0 reduce-scatter.6.cloned.1.call-start
  7.3 4.4 fusion.39
  11.7 2.0 fusion.40
  13.7 35.2 %all_gather.27 = f32[256,512]{1,0:T(8,128)} all-gather(f32[32,512]{1,0:T(8,128)S(1)} %pad_maximum_fusion.2), channel_id=1, replica_groups=mesh['row'=8,'col'=4] {'row'}, dimensions={0}, use_global_device_ids=true | all-gather | bytes 589824 | tf_op jit(solution)/shard_map/all_gather | solution.py:234
  49.0 0.0 reduce-scatter.6.cloned.1.call-update
  49.0 0.0 reduce-scatter.8.cloned.1.call-start
  49.1 1.1 fusion.41
  50.2 2.9 fusion.42
  53.1 7.6 %all_gather.28 = f32[256,512]{1,0:T(8,128)} all-gather(f32[64,512]{1,0:T(8,128)S(1)} %pad_maximum_fusion), channel_id=1, replica_groups=mesh['row'=8,'col'=4] {'col'}, dimensions={0}, use_global_device_ids=true | all-gather | bytes 655360 | tf_op jit(solution)/shard_map/all_gather | solution.py:228
  60.7 0.0 reduce-scatter.8.cloned.1.call-update
  60.8 0.0 all-gather.8.cloned.1.call-start
  60.8 11.0 %reduce-scatter.6.cloned.1.call-done = f32[64,512]{1,0:T(8,128)} async-done(((f32[256,512]{1,0:T(8,128)}), f32[64,512]{1,0:T(8,128)}) %reduce-scatter.6.cloned.1.call-update) | async-done | bytes 131088 | tf_op jit(solution)/shard_map/reduce_scatter | solution.py:237
  71.8 3.3 fusion.21
  75.2 0.0 all-gather.10.cloned.1.call-start
  75.2 62.7 %reduce-scatter.8.cloned.1.call-done = f32[32,512]{1,0:T(8,128)} async-done(((f32[256,512]{1,0:T(8,128)}), f32[32,512]{1,0:T(8,128)}) %reduce-scatter.8.cloned.1.call-update) | async-done | bytes 65552 | tf_op jit(solution)/shard_map/reduce_scatter | solution.py:231
  137.9 4.8 multiply_subtract_fusion.1
  142.7 0.0 all-gather.10.cloned.1.call-update
  142.7 0.0 all-gather.12.cloned.1.call-start
  142.8 0.7 pad_maximum_fusion.1
  143.4 0.0 all-gather.12.cloned.1.call-update
  143.5 0.0 reduce-scatter.12.cloned.1.call-start
  143.5 18.1 %all-gather.8.cloned.1.call-done.left_ref = f32[256,2048]{1,0:T(8,128)} async-done(((f32[64,2048]{1,0:T(8,128)}), f32[256,2048]{1,0:T(8,128)}) %all-gather.8.cloned.1.call-update) | async-done | bytes 2097168 | tf_op jit(solution)/shard_map/all_gather | solution.py:256
  161.6 75.4 %all-gather.10.cloned.1.call-done.right_ref = f32[256,4096]{1,0:T(8,128)} async-done(((f32[32,4096]{1,0:T(8,128)}), f32[256,4096]{1,0:T(8,128)}) %all-gather.10.cloned.1.call-update) | async-done | bytes 4194320 | tf_op jit(solution)/shard_map/all_gather | solution.py:255
  237.0 2.2 copy-done.9
  239.1 1.6 copy-done.13
  240.7 20.2 %shard_map.239 = f32[512,2048]{1,0:T(8,128)S(1)} custom-call(bf16[512,2048]{1,0:T(8,128)(2,1)S(1)} %copy-done.11, f32[256,2048]{1,0:T(8,128)S(1)} %copy-done.13, f32[256,4096]{1,0:T(8,128)S(1)} %copy-done.9, bf16[2048,4096]{1,0:T(8,128)(2,1)} %weight_ref.5), custom_call_target="tpu_custom_call" | custom-call | flops 10737418240 | bytes 12582912 | tf_op jit(solution)/shard_map/pallas_call | solution.py:109
  260.9 1.9 copy-done.5
  262.9 0.0 reduce-scatter.10.cloned.1.call-start
  263.0 2.2 copy-done.10
  265.1 1.6 copy-done.14
  266.7 20.1 %shard_map.236 = f32[512,2048]{1,0:T(8,128)S(1)} custom-call(bf16[512,2048]{1,0:T(8,128)(2,1)S(1)} %copy-done.11, f32[256,2048]{1,0:T(8,128)S(1)} %copy-done.14, f32[256,4096]{1,0:T(8,128)S(1)} %copy-done.10, bf16[2048,4096]{1,0:T(8,128)(2,1)} %weight_ref.5), custom_call_target="tpu_custom_call" | custom-call | flops 10737418240 | bytes 12582912 | tf_op jit(solution)/shard_map/pallas_call | solution.py:109
  286.8 2.0 copy-done.4
  288.9 0.0 reduce-scatter.10.cloned.1.call-update
  288.9 0.0 all-gather.18.cloned.1.call-start
  288.9 1.5 copy-done.16
  290.4 0.1 copy-done.20
  290.5 0.0 copy-done.21
  290.5 3.1 multiply_subtract_fusion
  293.7 0.2 all-gather.16.cloned.1.call-start
  293.9 4.8 fusion.13
  298.7 0.0 all-gather.16.cloned.1.call-update
  298.8 0.0 all-gather.20.cloned.1.call-start
  298.8 0.0 all-gather.12.cloned.1.call-done.k_ref.v_ref
  298.8 70.1 %reduce-scatter.12.cloned.1.call-done.q_ref = f32[64,2048]{1,0:T(8,128)} async-done(((f32[512,2048]{1,0:T(8,128)}), f32[64,2048]{1,0:T(8,128)}) %reduce-scatter.12.cloned.1.call-update) | async-done | bytes 524304 | tf_op jit(solution)/shard_map/reduce_scatter | solution.py:265
  368.9 1.2 copy-done.2
  370.2 1.0 copy-done.7
  371.2 4.2 shard_map.240
  375.4 0.0 all-gather.20.cloned.1.call-update
  375.4 0.0 all-gather.14.cloned.1.call-start
  375.5 85.1 %reduce-scatter.10.cloned.1.call-done.q_ref = f32[64,2048]{1,0:T(8,128)} async-done(((f32[512,2048]{1,0:T(8,128)}), f32[64,2048]{1,0:T(8,128)}) %reduce-scatter.10.cloned.1.call-update) | async-done | bytes 524304 | tf_op jit(solution)/shard_map/reduce_scatter | solution.py:265
  460.5 1.2 copy-done.3
  461.8 1.0 copy-done.6
  462.8 4.2 shard_map.237
  467.0 0.0 reduce-scatter.14.cloned.1.call-start
  467.1 17.8 %all-gather.18.cloned.1.call-done.right_ref = f32[256,2048]{1,0:T(8,128)} async-done(((f32[64,2048]{1,0:T(8,128)}), f32[256,2048]{1,0:T(8,128)}) %all-gather.18.cloned.1.call-update) | async-done | bytes 2097168 | tf_op jit(solution)/shard_map/all_gather | solution.py:258
  484.9 75.5 %all-gather.16.cloned.1.call-done.left_ref = f32[256,4096]{1,0:T(8,128)} async-done(((f32[32,4096]{1,0:T(8,128)}), f32[256,4096]{1,0:T(8,128)}) %all-gather.16.cloned.1.call-update) | async-done | bytes 4194320 | tf_op jit(solution)/shard_map/all_gather | solution.py:257
  560.4 2.2 copy-done.8
  562.6 1.6 copy-done.12
  564.2 32.6 %shard_map.238 = bf16[4096,2048]{1,0:T(8,128)(2,1)} custom-call(f32[256,4096]{1,0:T(8,128)S(1)} %copy-done.8, f32[256,2048]{1,0:T(8,128)S(1)} %copy-done.12, bf16[4096,2048]{1,0:T(8,128)(2,1)} %weight_ref.4), custom_call_target="tpu_custom_call" | custom-call | flops 12884901888 | bytes 33554432 | tf_op jit(solution)/shard_map/pallas_call | solution.py:137
  596.8 13.9 %all-gather.20.cloned.1.call-done = bf16[512,2048]{1,0:T(8,128)(2,1)} async-done(((bf16[64,2048]{1,0:T(8,128)(2,1)}), bf16[512,2048]{1,0:T(8,128)(2,1)}) %all-gather.20.cloned.1.call-update) | async-done | bytes 2097168 | tf_op jit(solution)/shard_map/all_gather | solution.py:285
  610.7 10.5 %fusion = f32[512,2048]{1,0:T(8,128)} fusion(bf16[512,2048]{1,0:T(8,128)(2,1)} %all-gather.20.cloned.1.call-done, bf16[4096,2048]{1,0:T(8,128)(2,1)} %shard_map.238), kind=kOutput, calls=%fused_computation | convolution fusion | flops 4294967296 | bytes 14680064 | tf_op jit(solution)/shard_map/dot_general | solution.py:294
  621.2 39.3 %all-gather.14.cloned.1.call-done = bf16[512,2048]{1,0:T(8,128)(2,1)} async-done(((bf16[64,2048]{1,0:T(8,128)(2,1)}), bf16[512,2048]{1,0:T(8,128)(2,1)}) %all-gather.14.cloned.1.call-update) | async-done | bytes 2097168 | tf_op jit(solution)/shard_map/all_gather | solution.py:285
  660.5 11.8 %fusion.4 = f32[512,2048]{1,0:T(8,128)} fusion(f32[512,2048]{1,0:T(8,128)} %fusion, bf16[512,2048]{1,0:T(8,128)(2,1)} %all-gather.14.cloned.1.call-done, bf16[4096,2048]{1,0:T(8,128)(2,1)} %shard_map.238), kind=kOutput, calls=%fused_computation.4 | convolution fusion | flops 4296015872 | bytes 18874368 | tf_op jit(solution)/shard_map/dot_general | solution.py:294
  672.3 43.3 %reduce-scatter.14.cloned.1.call-done = f32[128,2048]{1,0:T(8,128)} async-done(((f32[512,2048]{1,0:T(8,128)}), f32[128,2048]{1,0:T(8,128)}) %reduce-scatter.14.cloned.1.call-update) | async-done | bytes 1048592 | tf_op jit(solution)/shard_map/reduce_scatter | solution.py:301
  (42 shorter events, 0.2 us)
Async XLA Ops:
  7.2 41.9 %copy-start = (f32[256,2048]{1,0:T(8,128)S(1)}, f32[256,2048]{1,0:T(8,128)}, u32[]{:S(2)}) copy-start(f32[256,2048]{1,0:T(8,128)} %param.21) | copy-start | bytes 6291460
  7.2 4.5 copy-start.18
  7.2 64.7 %reduce-scatter.6.cloned.1.call-start = ((), (), s32[]{:S(2)}) async-start(), calls=%async_computation.5 | async-start | bytes 655360 | tf_op jit(solution)/shard_map/reduce_scatter | solution.py:237
  7.2 4.5 copy-start.15
  7.3 41.8 %copy-start.19 = (f32[2048,64]{0,1:T(8,128)S(1)}, f32[2048,64]{0,1:T(8,128)}, u32[]{:S(2)}) copy-start(f32[2048,64]{0,1:T(8,128)} %param.30) | copy-start | bytes 1572868
  49.0 88.9 %reduce-scatter.8.cloned.1.call-start = ((), (), s32[]{:S(2)}) async-start(), calls=%async_computation.6 | async-start | bytes 589824 | tf_op jit(solution)/shard_map/reduce_scatter | solution.py:231
  50.2 87.7 %copy-start.17 = (f32[32,4096]{1,0:T(8,128)S(1)}, f32[32,4096]{1,0:T(8,128)}, u32[]{:S(2)}) copy-start(f32[32,4096]{1,0:T(8,128)} %param.31) | copy-start | bytes 1572868
  60.8 100.8 %all-gather.8.cloned.1.call-start = ((), (), s32[]{:S(2)}) async-start(), calls=%async_computation.7 | async-start | bytes 2621440 | tf_op jit(solution)/shard_map/all_gather | solution.py:256
  75.1 67.6 %copy-start.23 = (bf16[128,256]{1,0:T(8,128)(2,1)S(1)}, bf16[128,256]{1,0:T(8,128)(2,1)}, u32[]{:S(2)}) copy-start(bf16[128,256]{1,0:T(8,128)(2,1)} %param.29) | copy-start | bytes 196612
  75.1 67.6 %copy-start.24 = (bf16[128,256]{1,0:T(8,128)(2,1)S(1)}, bf16[128,256]{1,0:T(8,128)(2,1)}, u32[]{:S(2)}) copy-start(bf16[128,256]{1,0:T(8,128)(2,1)} %param.28) | copy-start | bytes 196612
  75.1 161.8 %copy-start.11 = (bf16[512,2048]{1,0:T(8,128)(2,1)S(1)}, bf16[512,2048]{1,0:T(8,128)(2,1)}, u32[]{:S(2)}) copy-start(bf16[512,2048]{1,0:T(8,128)(2,1)} %x_ref.3) | copy-start | bytes 6291460
  75.2 161.8 %all-gather.10.cloned.1.call-start = ((), (), s32[]{:S(2)}) async-start(), calls=%async_computation.8 | async-start | bytes 4718592 | tf_op jit(solution)/shard_map/all_gather | solution.py:255
  142.7 156.1 %all-gather.12.cloned.1.call-start = ((), (), s32[]{:S(2)}) async-start(), calls=%async_computation.10 | async-start | bytes 1179648 | tf_op jit(solution)/shard_map/all_gather | solution.py:259
  143.5 225.5 %reduce-scatter.12.cloned.1.call-start = ((), (), s32[]{:S(2)}) async-start(), calls=%async_computation.14 | async-start | bytes 4718592 | tf_op jit(solution)/shard_map/reduce_scatter | solution.py:265
  237.0 2.2 copy-start.9
  239.1 1.6 copy-start.13
  260.9 2.0 copy-start.5
  262.9 197.6 %reduce-scatter.10.cloned.1.call-start = ((), (), s32[]{:S(2)}) async-start(), calls=%async_computation.9 | async-start | bytes 4718592 | tf_op jit(solution)/shard_map/reduce_scatter | solution.py:265
  263.0 2.2 copy-start.10
  265.1 1.6 copy-start.14
  286.8 2.0 copy-start.4
  288.9 1.6 copy-start.16
  288.9 1.7 copy-start.20
  288.9 1.7 copy-start.21
  288.9 5.0 copy-start.22
  288.9 196.0 %all-gather.18.cloned.1.call-start = ((), (), s32[]{:S(2)}) async-start(), calls=%async_computation.13 | async-start | bytes 2621440 | tf_op jit(solution)/shard_map/all_gather | solution.py:258
  293.7 266.8 %all-gather.16.cloned.1.call-start = ((), (), s32[]{:S(2)}) async-start(), calls=%async_computation.12 | async-start | bytes 4718592 | tf_op jit(solution)/shard_map/all_gather | solution.py:257
  298.8 311.9 %all-gather.20.cloned.1.call-start = ((), (), s32[]{:S(2)}) async-start(), calls=%async_computation.15 | async-start | bytes 2359296 | tf_op jit(solution)/shard_map/all_gather | solution.py:285
  368.9 1.2 copy-start.2
  370.2 1.0 copy-start.7
  375.4 285.1 %all-gather.14.cloned.1.call-start = ((), (), s32[]{:S(2)}) async-start(), calls=%async_computation.11 | async-start | bytes 2359296 | tf_op jit(solution)/shard_map/all_gather | solution.py:285
  460.5 1.2 copy-start.3
  461.8 1.0 copy-start.6
  467.0 248.5 %reduce-scatter.14.cloned.1.call-start = ((), (), s32[]{:S(2)}) async-start(), calls=%async_computation.16 | async-start | bytes 5242880 | tf_op jit(solution)/shard_map/reduce_scatter | solution.py:301
  560.4 2.2 copy-start.8
  562.6 1.6 copy-start.12
  660.5 55.1 %copy-start.1 = (f32[256,2048]{1,0:T(8,128)S(1)}, f32[256,2048]{1,0:T(8,128)}, u32[]{:S(2)}) copy-start(f32[256,2048]{1,0:T(8,128)} %param.21) | copy-start | bytes 6291460
Sparse Core Ops, SparseCore 0:
  49.1 22.6 reduce-scatter.5
  75.2 62.6 reduce-scatter.7
  140.0 21.5 all-gather.7
  164.1 72.7 all-gather.9
  239.5 38.8 all-gather.11
  281.8 87.0 reduce-scatter.11
  372.6 87.9 reduce-scatter.9
  462.7 22.1 all-gather.17
  487.6 72.7 all-gather.15
  563.0 47.6 all-gather.19
  612.8 47.6 all-gather.13
  672.4 43.1 reduce-scatter.13

commit v2 on v1

--- a/solution.py
+++ b/solution.py
@@ -197,6 +197,17 @@
             transcendentals=rows * width // head_dim * positions,
         ),
     )(query_rows, keys, values)
+
+
+def exchange_sum(value, axis):
+    count = lax.axis_size(axis)
+    blocks = value.reshape(count, value.shape[0] // count, value.shape[1])
+    received = lax.all_to_all(blocks, axis, 0, 0)
+    return jnp.sum(received.astype(jnp.float32), axis=0)
+
+
+def scatter_sum(value, axis):
+    return lax.psum_scatter(value, axis, scatter_dimension=0, tiled=True)
 
 
 def local(
@@ -228,13 +239,13 @@
     input_every = lax.all_gather(
         jnp.concatenate((input_turned, outcot_turned), axis=1), "col", axis=0, tiled=True
     )
-    input_rank = lax.psum_scatter(input_every, "row", scatter_dimension=0, tiled=True)
+    input_rank = exchange_sum(input_every, "row")
     cotan_turned = turned_product(query_right, query_cotangent)
     attn_turned = turned_product(output_left.T, training_attention)
     cotan_every = lax.all_gather(
         jnp.concatenate((cotan_turned, attn_turned), axis=1), "row", axis=0, tiled=True
     )
-    cotan_rank = lax.psum_scatter(cotan_every, "col", scatter_dimension=0, tiled=True)
+    cotan_rank = exchange_sum(cotan_every, "col")
     rows = training_input.shape[0]
     query_left_gradient = adapter_scale * high_product(cotan_rank[:, :rows], training_input).T
     query_right_gradient = adapter_scale * high_product(input_rank[:, :rows], query_cotangent)
@@ -262,7 +273,7 @@
     key_heads = cache_keys.shape[1] // HEAD_DIM
     width = query_weight.shape[1] // key_heads
     queries = [
-        lax.psum_scatter(
+        (exchange_sum if head % 2 else scatter_sum)(
             project_merged(
                 adapter_scale,
                 rollout_input,
@@ -273,8 +284,6 @@
                 width,
             ),
             "row",
-            scatter_dimension=0,
-            tiled=True,
         )
         for head in range(key_heads)
     ]
@@ -298,7 +307,7 @@
         )
         for head in range(key_heads)
     )
-    rollout_output = lax.psum_scatter(portion, "col", scatter_dimension=0, tiled=True)
+    rollout_output = exchange_sum(portion.astype(jnp.bfloat16), "col")
     return (
         stepped_query_left,
         new_query_right,

time: 724 us -> 622 us (0.86)
  waiting for transfers between devices: 512 us -> 344 us
  blocking collectives: 42.9 us -> 101 us
    reduce_scatter x5 -> x1, waiting for transfers between devices: 272 us -> 14.6 us  [scatter_sum(): return lax.psum_scatter(value, axis, scatter_dimension=0, tiled=True)]
    all_to_all x0 -> x1, waiting for transfers between devices: none -> 111 us  [exchange_sum(): received = lax.all_to_all(blocks, axis, 0, 0)]
    all_to_all x0 -> x3, blocking collectives: none -> 60.5 us  [exchange_sum(): received = lax.all_to_all(blocks, axis, 0, 0)]
    all_gather x1, waiting for transfers between devices: 18.1 us -> 0.02 us  [local(): lax.all_gather(stepped_query_left.T, 'col', axis=0, tiled=True)]
    unnamed x50 -> x44, local copies, waits for them, and re-layouts: 21.5 us -> 19.8 us
  transfers between devices with their start and end apart: 12 -> 9, of which waited for: 11 -> 7; matrix products, arithmetic and copies ran while one was open for 4% -> 5% of each run, Pallas kernels for 11% -> 13%
where the time goes in v2:
time: 622 us; the launch traced here: 620 us
  waiting for transfers between devices  344 us (55%)
  blocking collectives  101 us (16%)
  Pallas kernels  81.3 us (13%)
  matrix products  48.1 us (8%)
  local copies, waits for them, and re-layouts  19.8 us (3%)
  between operations  14.4 us (2%)
    all_to_all x1, waiting for transfers between devices, exchange_sum(): received = lax.all_to_all(blocks, axis, 0, 0)  111 us
    all_gather x1, waiting for transfers between devices, local(): lax.all_gather(new_output_left.T, 'row', axis=0, tiled=True)  75.4 us
    all_gather x1, waiting for transfers between devices, local(): lax.all_gather(new_query_right, 'row', axis=0, tiled=True)  71.4 us
    all_to_all x3, blocking collectives, exchange_sum(): received = lax.all_to_all(blocks, axis, 0, 0)  60.5 us
    all_gather x2, waiting for transfers between devices, local(): lax.all_gather(attend(queries[head], cache_all, cache_all, head, key_head...  53.3 us
    pallas_call x2, Pallas kernels, project_merged(): pl.pallas_call(functools.partial(project_kernel, scale), grid=(width // t...  40.3 us
    all_gather x1, blocking collectives, local(): lax.all_gather(jnp.concatenate((cotan_turned, attn_turned), axis=1), 'row...  33 us
    pallas_call x1, Pallas kernels, merge_weight(): pl.pallas_call(functools.partial(merge_kernel, scale), grid=(width // til...  32.6 us
  transfers between devices with their start and end apart: 9, of which 7 were waited for; matrix products, arithmetic and copies ran while one was open for 5% of the time, Pallas kernels for 13%

profile of v2, /device:TPU:0, one launch (start us, length us, event | category | flops | bytes accessed | tf_op | source)
XLA Modules:
  0.0 619.5 jit_solution(3466412927092333430)
XLA Ops:
  7.2 0.0 copy-start
  7.2 0.0 all-gather.8.cloned.1.call-start
  7.2 0.0 copy-start.14
  7.3 4.4 fusion.38
  11.7 2.0 fusion.39
  13.7 33.0 %all_gather.27 = f32[256,512]{1,0:T(8,128)S(1)} all-gather(f32[32,512]{1,0:T(8,128)S(1)} %pad_maximum_fusion.2), channel_id=1, replica_groups=mesh['row'=8,'col'=4] {'row'}, dimensions={0}, use_global_device_ids=true | all-gather | bytes 589824 | tf_op jit(solution)/shard_map/all_gather | solution.py:245
  46.8 11.4 %all_to_all.20 = f32[4,64,512]{2,1,0:T(8,128)S(1)} all-to-all(f32[4,64,512]{2,1,0:T(8,128)S(1)} %bitcast.68), channel_id=1, replica_groups=mesh['row'=8,'col'=4] {'col'}, dimensions={0} | all-to-all | bytes 1048576 | tf_op jit(solution)/shard_map/all_to_all | solution.py:205
  58.2 3.3 fusion.20
  61.5 0.0 all-gather.8.cloned.1.call-update
  61.5 0.0 all-gather.10.cloned.1.call-start
  61.5 2.2 fusion.40
  63.7 2.9 fusion.41
  66.6 7.7 %all_gather.28 = f32[256,512]{1,0:T(8,128)S(1)} all-gather(f32[64,512]{1,0:T(8,128)S(1)} %pad_maximum_fusion), channel_id=1, replica_groups=mesh['row'=8,'col'=4] {'col'}, dimensions={0}, use_global_device_ids=true | all-gather | bytes 655360 | tf_op jit(solution)/shard_map/all_gather | solution.py:239
  74.3 20.9 %all_to_all.21 = f32[8,32,512]{2,1,0:T(8,128)} all-to-all(f32[8,32,512]{2,1,0:T(8,128)S(1)} %bitcast.66), channel_id=1, replica_groups=mesh['row'=8,'col'=4] {'row'}, dimensions={0} | all-to-all | bytes 1048576 | tf_op jit(solution)/shard_map/all_to_all | solution.py:205
  95.2 1.1 reduce_sum.37
  96.3 4.8 multiply_subtract_fusion.1
  101.1 0.0 all-gather.10.cloned.1.call-update
  101.1 0.0 all-gather.12.cloned.1.call-start
  101.2 0.7 pad_maximum_fusion.1
  101.8 0.0 all-gather.12.cloned.1.call-update
  101.9 0.0 reduce-scatter.2.cloned.1.call-start
  101.9 0.0 all-gather.8.cloned.1.call-done.left_ref
  101.9 71.4 %all-gather.10.cloned.1.call-done.right_ref = f32[256,4096]{1,0:T(8,128)} async-done(((f32[32,4096]{1,0:T(8,128)}), f32[256,4096]{1,0:T(8,128)}) %all-gather.10.cloned.1.call-update) | async-done | bytes 4194320 | tf_op jit(solution)/shard_map/all_gather | solution.py:266
  173.3 2.2 copy-done.8
  175.5 1.6 copy-done.12
  177.1 20.1 %shard_map.236 = f32[512,2048]{1,0:T(8,128)S(1)} custom-call(bf16[512,2048]{1,0:T(8,128)(2,1)S(1)} %copy-done.10, f32[256,2048]{1,0:T(8,128)S(1)} %copy-done.12, f32[256,4096]{1,0:T(8,128)S(1)} %copy-done.8, bf16[2048,4096]{1,0:T(8,128)(2,1)} %weight_ref.5), custom_call_target="tpu_custom_call" | custom-call | flops 10737418240 | bytes 12582912 | tf_op jit(solution)/shard_map/pallas_call | solution.py:109
  197.2 1.9 copy-done.4
  199.2 0.0 reduce-scatter.2.cloned.1.call-update
  199.2 0.0 all-gather.18.cloned.1.call-start
  199.2 1.0 copy-done.17
  200.2 3.7 multiply_subtract_fusion
  203.9 0.0 all-gather.18.cloned.1.call-update
  204.0 2.2 copy-done.9
  206.2 1.6 copy-done.13
  207.8 20.3 %shard_map.239 = f32[512,2048]{1,0:T(8,128)S(1)} custom-call(bf16[512,2048]{1,0:T(8,128)(2,1)S(1)} %copy-done.10, f32[256,2048]{1,0:T(8,128)S(1)} %copy-done.13, f32[256,4096]{1,0:T(8,128)S(1)} %copy-done.9, bf16[2048,4096]{1,0:T(8,128)(2,1)} %weight_ref.5), custom_call_target="tpu_custom_call" | custom-call | flops 10737418240 | bytes 12582912 | tf_op jit(solution)/shard_map/pallas_call | solution.py:109
  228.1 1.9 copy-done.5
  230.0 4.9 all-to-all-start.2
  234.9 0.0 all-gather.16.cloned.1.call-start
  235.0 4.6 fusion.12
  239.6 0.0 all-gather.16.cloned.1.call-update
  239.6 0.0 all-gather.20.cloned.1.call-start
  239.6 111.3 %all-to-all-done.2 = f32[8,64,2048]{2,1,0:T(8,128)} async-done(((f32[8,64,2048]{2,1,0:T(8,128)}), f32[8,64,2048]{2,1,0:T(8,128)}, u32[]{:S(2)}, u32[]{:S(2)}) %all-to-all-start.2) | async-done | bytes 4194336 | tf_op jit(solution)/shard_map/all_to_all | solution.py:205
  350.9 2.5 reduce_sum.38.q_ref
  353.4 0.0 all-gather.12.cloned.1.call-done.k_ref.v_ref
  353.5 1.2 copy-done.2
  354.7 4.2 shard_map.240
  358.9 0.0 all-gather.20.cloned.1.call-update
  358.9 0.0 all-gather.14.cloned.1.call-start
  359.0 14.6 %reduce-scatter.2.cloned.1.call-done.q_ref = f32[64,2048]{1,0:T(8,128)} async-done(((f32[512,2048]{1,0:T(8,128)}), f32[64,2048]{1,0:T(8,128)}) %reduce-scatter.2.cloned.1.call-update) | async-done | bytes 524304 | tf_op jit(solution)/shard_map/reduce_scatter | solution.py:210
  373.6 1.2 copy-done.3
  374.8 1.0 copy-done.6
  375.8 4.2 shard_map.237
  380.0 0.0 all-gather.14.cloned.1.call-update
  380.1 17.7 %all-gather.18.cloned.1.call-done.right_ref = f32[256,2048]{1,0:T(8,128)} async-done(((f32[64,2048]{1,0:T(8,128)}), f32[256,2048]{1,0:T(8,128)}) %all-gather.18.cloned.1.call-update) | async-done | bytes 2097168 | tf_op jit(solution)/shard_map/all_gather | solution.py:269
  397.8 75.4 %all-gather.16.cloned.1.call-done.left_ref = f32[256,4096]{1,0:T(8,128)} async-done(((f32[32,4096]{1,0:T(8,128)}), f32[256,4096]{1,0:T(8,128)}) %all-gather.16.cloned.1.call-update) | async-done | bytes 4194320 | tf_op jit(solution)/shard_map/all_gather | solution.py:268
  473.2 2.2 copy-done.7
  475.4 1.6 copy-done.11
  477.0 32.6 %shard_map.238 = bf16[4096,2048]{1,0:T(8,128)(2,1)} custom-call(f32[256,4096]{1,0:T(8,128)S(1)} %copy-done.7, f32[256,2048]{1,0:T(8,128)S(1)} %copy-done.11, bf16[4096,2048]{1,0:T(8,128)(2,1)} %weight_ref.4), custom_call_target="tpu_custom_call" | custom-call | flops 12884901888 | bytes 33554432 | tf_op jit(solution)/shard_map/pallas_call | solution.py:137
  509.5 14.0 %all-gather.20.cloned.1.call-done = bf16[512,2048]{1,0:T(8,128)(2,1)} async-done(((bf16[64,2048]{1,0:T(8,128)(2,1)}), bf16[512,2048]{1,0:T(8,128)(2,1)}) %all-gather.20.cloned.1.call-update) | async-done | bytes 2097168 | tf_op jit(solution)/shard_map/all_gather | solution.py:294
  523.5 10.5 %fusion = f32[512,2048]{1,0:T(8,128)} fusion(bf16[512,2048]{1,0:T(8,128)(2,1)} %all-gather.20.cloned.1.call-done, bf16[4096,2048]{1,0:T(8,128)(2,1)} %shard_map.238), kind=kOutput, calls=%fused_computation | convolution fusion | flops 4294967296 | bytes 14680064 | tf_op jit(solution)/shard_map/dot_general | solution.py:303
  534.0 39.3 %all-gather.14.cloned.1.call-done = bf16[512,2048]{1,0:T(8,128)(2,1)} async-done(((bf16[64,2048]{1,0:T(8,128)(2,1)}), bf16[512,2048]{1,0:T(8,128)(2,1)}) %all-gather.14.cloned.1.call-update) | async-done | bytes 2097168 | tf_op jit(solution)/shard_map/all_gather | solution.py:294
  573.3 9.8 %add_convert_fusion = bf16[512,2048]{1,0:T(8,128)(2,1)S(1)} fusion(f32[512,2048]{1,0:T(8,128)} %fusion, bf16[512,2048]{1,0:T(8,128)(2,1)} %all-gather.14.cloned.1.call-done, bf16[4096,2048]{1,0:T(8,128)(2,1)} %shard_map.238), kind=kOutput, calls=%fused_computation.5 | convolution fusion | flops 4297064448 | bytes 16777216 | tf_op jit(solution)/shard_map/dot_general | solution.py:303
  583.1 28.2 %all_to_all.22 = bf16[4,128,2048]{2,1,0:T(8,128)(2,1)S(1)} all-to-all(bf16[4,128,2048]{2,1,0:T(8,128)(2,1)S(1)} %bitcast.67), channel_id=1, replica_groups=mesh['row'=8,'col'=4] {'col'}, dimensions={0} | all-to-all | bytes 4194304 | tf_op jit(solution)/shard_map/all_to_all | solution.py:205
  611.3 1.4 convert_reduce_fusion
  (33 shorter events, 0.1 us)
Async XLA Ops:
  7.2 51.0 %copy-start = (f32[256,2048]{1,0:T(8,128)S(1)}, f32[256,2048]{1,0:T(8,128)}, u32[]{:S(2)}) copy-start(f32[256,2048]{1,0:T(8,128)} %param.21) | copy-start | bytes 6291460
  7.2 4.5 copy-start.16
  7.2 94.7 %all-gather.8.cloned.1.call-start = ((), (), s32[]{:S(2)}) async-start(), calls=%async_computation.5 | async-start | bytes 2621440 | tf_op jit(solution)/shard_map/all_gather | solution.py:267
  7.2 4.4 copy-start.14
  61.5 34.8 %copy-start.15 = (f32[32,4096]{1,0:T(8,128)S(1)}, f32[32,4096]{1,0:T(8,128)}, u32[]{:S(2)}) copy-start(f32[32,4096]{1,0:T(8,128)} %param.31) | copy-start | bytes 1572868
  61.5 111.8 %all-gather.10.cloned.1.call-start = ((), (), s32[]{:S(2)}) async-start(), calls=%async_computation.6 | async-start | bytes 4718592 | tf_op jit(solution)/shard_map/all_gather | solution.py:266
  74.3 26.9 %copy-start.20 = (bf16[128,256]{1,0:T(8,128)(2,1)S(1)}, bf16[128,256]{1,0:T(8,128)(2,1)}, u32[]{:S(2)}) copy-start(bf16[128,256]{1,0:T(8,128)(2,1)} %param.29) | copy-start | bytes 196612
  74.3 26.9 %copy-start.21 = (bf16[128,256]{1,0:T(8,128)(2,1)S(1)}, bf16[128,256]{1,0:T(8,128)(2,1)}, u32[]{:S(2)}) copy-start(bf16[128,256]{1,0:T(8,128)(2,1)} %param.28) | copy-start | bytes 196612
  74.3 99.0 %copy-start.10 = (bf16[512,2048]{1,0:T(8,128)(2,1)S(1)}, bf16[512,2048]{1,0:T(8,128)(2,1)}, u32[]{:S(2)}) copy-start(bf16[512,2048]{1,0:T(8,128)(2,1)} %x_ref.3) | copy-start | bytes 6291460
  101.1 252.4 %all-gather.12.cloned.1.call-start = ((), (), s32[]{:S(2)}) async-start(), calls=%async_computation.8 | async-start | bytes 1179648 | tf_op jit(solution)/shard_map/all_gather | solution.py:270
  101.9 271.7 %reduce-scatter.2.cloned.1.call-start = ((), (), s32[]{:S(2)}) async-start(), calls=%async_computation.7 | async-start | bytes 4718592 | tf_op jit(solution)/shard_map/reduce_scatter | solution.py:210
  173.3 2.2 copy-start.8
  175.5 1.6 copy-start.12
  197.2 2.0 copy-start.4
  199.2 1.0 copy-start.17
  199.2 198.6 %all-gather.18.cloned.1.call-start = ((), (), s32[]{:S(2)}) async-start(), calls=%async_computation.11 | async-start | bytes 2621440 | tf_op jit(solution)/shard_map/all_gather | solution.py:269
  203.9 2.2 copy-start.9
  206.2 1.6 copy-start.13
  228.0 1.9 copy-start.5
  230.0 5.0 copy-start.18
  230.0 5.0 copy-start.19
  230.0 121.0 %all-to-all-start.2 = ((f32[8,64,2048]{2,1,0:T(8,128)}), f32[8,64,2048]{2,1,0:T(8,128)}, u32[]{:S(2)}, u32[]{:S(2)}) async-start(f32[8,64,2048]{2,1,0:T(8,128)} %bitcast.64), calls=%async_computation.3 | async-start | bytes 8388608 | tf_op jit(solution)/shard_map/all_to_all | solution.py:205
  234.9 238.3 %all-gather.16.cloned.1.call-start = ((), (), s32[]{:S(2)}) async-start(), calls=%async_computation.10 | async-start | bytes 4718592 | tf_op jit(solution)/shard_map/all_gather | solution.py:268
  239.6 283.9 %all-gather.20.cloned.1.call-start = ((), (), s32[]{:S(2)}) async-start(), calls=%async_computation.12 | async-start | bytes 2359296 | tf_op jit(solution)/shard_map/all_gather | solution.py:294
  353.5 1.2 copy-start.2
  358.9 214.4 %all-gather.14.cloned.1.call-start = ((), (), s32[]{:S(2)}) async-start(), calls=%async_computation.9 | async-start | bytes 2359296 | tf_op jit(solution)/shard_map/all_gather | solution.py:294
  373.6 1.2 copy-start.3
  374.8 1.0 copy-start.6
  473.2 2.2 copy-start.7
  475.4 1.6 copy-start.11
  573.3 39.4 %copy-start.1 = (f32[256,2048]{1,0:T(8,128)S(1)}, f32[256,2048]{1,0:T(8,128)}, u32[]{:S(2)}) copy-start(f32[256,2048]{1,0:T(8,128)} %param.21) | copy-start | bytes 6291460
Sparse Core Ops, SparseCore 0:
  61.6 23.3 all-gather.7
  101.2 72.0 all-gather.9
  176.0 38.7 all-gather.11
  218.4 155.1 reduce-scatter.1
  375.6 22.1 all-gather.17
  400.4 72.7 all-gather.15
  475.9 47.6 all-gather.19
  525.6 47.6 all-gather.13
